TPU v7x, 32 devices: a whole 2x2x4 slice. The times are simulated.
32 devices in a mesh: dp: 8 (over z, y), tensor: 4 (over x, core).
Axes of the slice: x: 2, y: 2, z: 4, core: 2. Of those that a mesh axis runs over, the one named last changes fastest.
Arguments:
- query: bfloat16 [64, 64, 128], P('dp', 'tensor'), may hold values from -8 to 8
- kv_pages: bfloat16 [560, 8, 2, 128, 128], P('dp', 'tensor'), may hold values from -8 to 8
- move_plan: int32 [8, 3, 12], P('dp'), may hold values from 0 to 69, as said below
- move_count: int32 [8], P('dp'), may hold values from 9 to 12
- block_table: int32 [64, 8], P('dp'), may hold values from 0 to 69, as said below
- seq_lens: int32 [64], P('dp'), may hold values from 1 to 1024
- out_weight: bfloat16 [8192, 8192], P('tensor', 'dp'), may hold values from -0.0625 to 0.0625
Outputs:
- new_pages: bfloat16 [560, 8, 2, 128, 128], P('dp', 'tensor')
- projected: bfloat16 [64, 8192], P(None, 'dp')
Inputs may be any that keep to these rules, and one draw needn't show every extreme that they name: `move_plan`: row 0 holds the device's own source slots, distinct within a device; row 1 target devices; row 2 target slots. Entries at or past the device's move_count are padding to be ignored. At most 2 valid moves go from one device to one device, and some pair has exactly 2. The (target device, target slot) pairs of all valid moves are distinct. `block_table`: all entries of the sequences of one device are distinct slots of that device; sequence s belongs to device s // 8.
All inputs are finite; a program needn't handle non-finite values.
Results may differ from a plain program's by a relative error of at most 0.0055.
Values may be sent and summed in bfloat16 or wider, within the bound.
No kernel may reach another device: no remote copies, remote signals or barrier semaphores. Data moves between devices by JAX's collectives and lax.ppermute only.
A program may use at most 128 MiB of HBM per device.

v0:
```python
import math
import jax
import jax.numpy as jnp
from jax import lax
from jax.sharding import PartitionSpec as P

HD = 128
BLOCK = 128
BLOCKS = 8
CAP = 2


def body(query, kv_pages, move_plan, move_count, block_table, seq_lens, out_weight):
    slots_here = kv_pages.shape[0]
    move_total = move_plan.shape[2]
    devices = lax.axis_size("dp")
    capacity = CAP
    holding_rows = devices * capacity
    move_list = move_plan[0]
    move_index = jnp.arange(move_total, dtype=jnp.int32)
    is_valid = move_index < move_count[0]
    target_dev = move_list[1]
    earlier = (
        (target_dev[:, None] == target_dev[None, :])
        & is_valid[None, :]
        & (move_index[None, :] < move_index[:, None])
    )
    dest_rank = jnp.sum(earlier.astype(jnp.int32), axis=1)
    send_row = jnp.where(is_valid, target_dev * capacity + dest_rank, -1)
    flat_pages = kv_pages.reshape(slots_here, -1)
    picked = flat_pages[move_list[0]]
    select = jnp.arange(holding_rows, dtype=jnp.int32)[:, None] == send_row[None, :]
    outgoing = jnp.dot(
        select.astype(jnp.bfloat16), picked, preferred_element_type=jnp.float32
    ).astype(jnp.bfloat16)
    outgoing = outgoing.reshape((holding_rows,) + kv_pages.shape[1:])
    out_slots = jnp.sum(select.astype(jnp.int32) * (move_list[2][None, :] + 1), axis=1) - 1
    slot_tags = out_slots.astype(jnp.float32).astype(jnp.bfloat16)
    arrived, arrived_tags = (
        lax.all_to_all(outgoing, "dp", split_axis=0, concat_axis=0, tiled=True),
        lax.all_to_all(slot_tags, "dp", split_axis=0, concat_axis=0, tiled=True),
    )
    incoming = arrived_tags.astype(jnp.float32).astype(jnp.int32)
    hit_table = jnp.arange(slots_here, dtype=jnp.int32)[:, None] == incoming[None, :]
    placed = jnp.dot(
        hit_table.astype(jnp.bfloat16),
        arrived.reshape(holding_rows, -1),
        preferred_element_type=jnp.float32,
    ).astype(jnp.bfloat16)
    written = jnp.any(hit_table, axis=1)
    new_pages = jnp.where(written[:, None], placed, flat_pages).reshape(kv_pages.shape)
    seq_here = query.shape[0]
    local_heads = new_pages.shape[1]
    head_dim = query.shape[2]
    group_size = query.shape[1] // local_heads
    context = BLOCKS * BLOCK
    gathered = new_pages[block_table]
    key_rows = jnp.transpose(gathered[:, :, :, 0], (0, 2, 1, 3, 4)).reshape(
        seq_here, local_heads, context, head_dim
    )
    value_rows = jnp.transpose(gathered[:, :, :, 1], (0, 2, 1, 3, 4)).reshape(
        seq_here, local_heads, context, head_dim
    )
    grouped = query.reshape(seq_here, local_heads, group_size, head_dim)
    score_scale = 1.0 / math.sqrt(HD)
    scores = (
        jnp.einsum("skgd,sktd->skgt", grouped, key_rows, preferred_element_type=jnp.float32)
        * score_scale
    )
    position = jnp.arange(context, dtype=jnp.int32)
    scores = jnp.where(position[None, None, None, :] < seq_lens[:, None, None, None], scores, -1e30)
    largest = jnp.max(scores, axis=-1, keepdims=True)
    expo = jnp.exp(scores - largest)
    weights = (expo / jnp.sum(expo, axis=-1, keepdims=True)).astype(jnp.bfloat16)
    mixed_heads = jnp.einsum(
        "skgt,sktd->skgd", weights, value_rows, preferred_element_type=jnp.float32
    )
    attention = mixed_heads.reshape(seq_here, local_heads * group_size * head_dim).astype(
        jnp.bfloat16
    )
    partial_sums = jnp.dot(
        lax.all_gather(attention, "dp", axis=0, tiled=True),
        out_weight,
        preferred_element_type=jnp.float32,
    )
    summed = lax.psum(partial_sums, "tensor")
    return (new_pages, summed.astype(jnp.bfloat16))


def solution(mesh):
    placed = (
        P("dp", "tensor", None),
        P("dp", "tensor", None, None, None),
        P("dp", None, None),
        P("dp"),
        P("dp", None),
        P("dp"),
        P("tensor", "dp"),
    )
    return jax.shard_map(
        body,
        mesh=mesh,
        in_specs=placed,
        out_specs=(P("dp", "tensor", None, None, None), P(None, "dp")),
        check_vma=False,
    )
```

profile of v0, /device:TPU:1, one launch (start us, length us, event | category | flops | bytes accessed | tf_op | source)
XLA Modules:
  0.0 194.9 jit_solution(8297206147046076033)
XLA Ops:
  0.6 0.0 copy-start
  0.6 0.7 slice_bitcast_fusion
  2.0 0.2 convert_reduce_fusion
  2.2 0.7 add_select_fusion
  2.8 0.1 select_reduce_fusion
  3.0 0.7 convert_element_type.79
  3.7 6.4 %all-to-all-start = ((bf16[8,2,1]{1,2,0:T(2,128)(2,1)}), bf16[8,2,1]{1,2,0:T(2,128)(2,1)S(1)}, u32[]{:S(2)}, u32[]{:S(2)}) async-start(bf16[8,2,1]{1,2,0:T(2,128)(2,1)} %convert_element_type.79), calls=%async_computation | async-start | bytes 8192 | tf_op jit(solution)/shard_map/all_to_all | solution.py:41
  10.0 0.7 fusion.16
  10.7 8.8 %pad.2 = bf16[72,512,128]{2,1,0:T(8,128)(2,1)} pad(bf16[70,512,128]{2,1,0:T(8,128)(2,1)} %bitcast.69, bf16[]{:T(256)} %constant.38), padding=0_2x0_0x0_0 | pad | bytes 18612226
  19.5 13.8 %copy.21 = bf16[9,8,512,128]{3,1,2,0:T(8,128)(2,1)} copy(bf16[9,8,512,128]{3,2,1,0:T(8,128)(2,1)} %bitcast.62) | data formatting | bytes 18874368
  33.3 7.8 %gather_fusion = bf16[12,65536]{1,0:T(8,128)(2,1)S(1)} fusion(bf16[70,65536]{1,0:T(8,128)(2,1)} %bitcast.59, s32[1024]{0:T(1024)S(1)} %pad_clamp_fusion.1), kind=kCustom, calls=%fused_computation | custom fusion | bytes 3145776 | tf_op jit(solution)/shard_map/gather | solution.py:31
  41.1 0.7 fusion.4
  41.8 0.0 copy-start.1
  41.8 0.0 copy-start.2
  41.8 1.9 copy.22
  43.7 0.0 all-to-all-done
  43.7 5.4 %all-to-all-start.1 = ((bf16[16,2,2,128,128]{4,3,2,1,0:T(8,128)(2,1)}), bf16[16,2,2,128,128]{4,3,2,1,0:T(8,128)(2,1)S(1)}, u32[]{:S(2)}, u32[]{:S(2)}) async-start(bf16[16,2,2,128,128]{4,3,2,1,0:T(8,128)(2,1)} %bitcast.24), calls=%async_computation.1 | async-start | bytes 4194304 | tf_op jit(solution)/shard_map/all_to_all | solution.py:40
  49.2 0.0 copy-done.1
  49.2 0.1 reshape.158
  49.3 0.0 copy-done.2
  49.3 0.1 iota_compare_fusion
  49.4 0.1 convert_element_type.72
  49.4 0.1 fusion.12
  49.5 46.5 %all-to-all-done.1 = bf16[16,2,2,128,128]{4,3,2,1,0:T(8,128)(2,1)S(1)} async-done(((bf16[16,2,2,128,128]{4,3,2,1,0:T(8,128)(2,1)}), bf16[16,2,2,128,128]{4,3,2,1,0:T(8,128)(2,1)S(1)}, u32[]{:S(2)}, u32[]{:S(2)}) %all-to-all-start.1) | async-done | bytes 2097184 | tf_op jit(solution)/shard_map/all_to_all | solution.py:40
  96.0 10.8 %fusion.1 = bf16[70,65536]{1,0:T(8,128)(2,1)} fusion(bf16[70,65536]{1,0:T(8,128)(2,1)} %bitcast.60, pred[70]{0:T(512)(128)(4,1)S(1)} %fusion.12, bf16[2,8,512,128]{3,2,1,0:T(8,128)(2,1)S(1)} %bitcast.70, s32[16]{0:T(128)S(1)} %convert_element_type.72), kind=kOutput, calls=%fused_computation.4 | convolution fusion | flops 155976800 | bytes 20447366 | tf_op jit(solution)/shard_map/dot_general | solution.py:45
  106.8 9.9 %copy.24 = bf16[9,8,512,128]{3,2,1,0:T(8,128)(2,1)} copy(bf16[9,8,512,128]{3,1,2,0:T(8,128)(2,1)} %bitcast.61) | data formatting | bytes 18874368
  116.7 8.4 %slice.29 = bf16[70,512,128]{2,1,0:T(8,128)(2,1)} slice(bf16[72,512,128]{2,1,0:T(8,128)(2,1)} %bitcast.63), slice={[0:70], [0:512], [0:128]} | slice | bytes 18350080
  125.1 9.1 %gather_fusion.1 = bf16[64,2,2,128,128]{4,3,2,1,0:T(8,128)(2,1)} fusion(bf16[70,2,2,128,128]{4,3,2,1,0:T(8,128)(2,1)} %bitcast.64, s32[1024]{0:T(1024)S(1)} %pad_clamp_fusion), kind=kCustom, calls=%fused_computation.1 | custom fusion | bytes 16777472 | tf_op jit(solution)/shard_map/gather | solution.py:57
  134.2 3.8 %fusion.17 = (bf16[8,8,2,1,128,128]{5,4,3,2,1,0:T(8,128)(2,1)S(1)}, bf16[8,8,2,1,128,128]{5,4,3,2,1,0:T(8,128)(2,1)S(1)}) fusion(bf16[8,8,2,2,128,128]{5,4,3,2,1,0:T(8,128)(2,1)} %bitcast.66), kind=kLoop, calls=%fused_computation.41 | loop fusion | bytes 16777216 | tf_op jit(solution)/shard_map/slice | solution.py:58
  138.1 0.6 copy.19
  138.6 0.0 copy-done
  138.7 1.2 fusion.8
  139.8 0.3 fusion.18
  140.1 2.2 %copy.20 = bf16[8,8,2,1,128,128]{5,4,1,2,0,3:T(8,128)(2,1)} copy(bf16[8,8,2,1,128,128]{5,4,3,2,1,0:T(8,128)(2,1)S(1)} %get-tuple-element.3) | data formatting | bytes 8388608
  142.3 2.9 %fusion.9 = bf16[1,8,16,128]{3,2,1,0:T(8,128)(2,1)S(1)} fusion(bf16[8,2,1024,128]{3,2,1,0:T(8,128)(2,1)} %bitcast.67, f32[8,2,8]{2,1,0:T(2,128)S(1)} %fusion.18, f32[8,2,8,1024]{3,2,1,0:T(8,128)S(1)} %fusion.8), kind=kOutput, calls=%fused_computation.15 | convolution fusion | flops 33965184 | bytes 4751872 | tf_op jit(solution)/shard_map/skgt,sktd->skgd/dot_general | solution.py:75
  145.3 25.4 %all_gather.3 = bf16[64,2048]{1,0:T(8,128)(2,1)S(1)} all-gather(bf16[8,2048]{1,0:T(8,128)(2,1)S(1)} %bitcast.71), channel_id=1, replica_groups=mesh['dp'=8,'tensor'=4] {'dp'}, dimensions={0}, use_global_device_ids=true | all-gather | bytes 294912 | tf_op jit(solution)/shard_map/all_gather | solution.py:82
  170.7 3.0 %fusion.19 = f32[64,1024]{1,0:T(8,128)S(1)} fusion(bf16[64,2048]{1,0:T(8,128)(2,1)S(1)} %all_gather.3, bf16[2048,1024]{1,0:T(8,128)(2,1)} %param.13), kind=kOutput, calls=%fused_computation.43 | convolution fusion | flops 268435456 | bytes 4718592 | tf_op jit(solution)/shard_map/dot_general | solution.py:81
  173.7 21.2 %all-reduce.1 = bf16[64,1024]{1,0:T(8,128)(2,1)} all-reduce(f32[64,1024]{1,0:T(8,128)S(1)} %fusion.19), channel_id=1, replica_groups=mesh['dp'=8,'tensor'=4] {'tensor'}, use_global_device_ids=true, to_apply=%region_5.6 | all-reduce | flops 65536 | bytes 393216 | tf_op jit(solution)/shard_map/psum | solution.py:86
  (7 shorter events, 0.1 us)
Async XLA Ops:
  0.6 138.0 %copy-start = (bf16[8,16,128]{2,1,0:T(8,128)(2,1)S(1)}, bf16[8,16,128]{2,1,0:T(8,128)(2,1)}, u32[]{:S(2)}) copy-start(bf16[8,16,128]{2,1,0:T(8,128)(2,1)} %param.7) | copy-start | bytes 98308
  3.7 40.1 %all-to-all-start = ((bf16[8,2,1]{1,2,0:T(2,128)(2,1)}), bf16[8,2,1]{1,2,0:T(2,128)(2,1)S(1)}, u32[]{:S(2)}, u32[]{:S(2)}) async-start(bf16[8,2,1]{1,2,0:T(2,128)(2,1)} %convert_element_type.79), calls=%async_computation | async-start | bytes 8192 | tf_op jit(solution)/shard_map/all_to_all | solution.py:41
  41.8 7.3 %copy-start.1 = (s32[8,8]{1,0:T(8,128)S(1)}, s32[8,8]{1,0:T(8,128)}, u32[]{:S(2)}) copy-start(s32[8,8]{1,0:T(8,128)} %param.11) | copy-start | bytes 772
  41.8 7.4 %copy-start.2 = (s32[8]{0:T(128)S(1)}, s32[8]{0:T(128)}, u32[]{:S(2)}) copy-start(s32[8]{0:T(128)} %param.12) | copy-start | bytes 100
  43.7 52.3 %all-to-all-start.1 = ((bf16[16,2,2,128,128]{4,3,2,1,0:T(8,128)(2,1)}), bf16[16,2,2,128,128]{4,3,2,1,0:T(8,128)(2,1)S(1)}, u32[]{:S(2)}, u32[]{:S(2)}) async-start(bf16[16,2,2,128,128]{4,3,2,1,0:T(8,128)(2,1)} %bitcast.24), calls=%async_computation.1 | async-start | bytes 4194304 | tf_op jit(solution)/shard_map/all_to_all | solution.py:40
where the time goes:
time: 196 us; the launch traced here: 195 us
  local copies, waits for them, and re-layouts  67.2 us (34%)
  blocking collectives  46.6 us (24%)
  waiting for transfers between devices  46.5 us (24%)
  matrix products  18.6 us (9%)
  starting transfers between devices  11.8 us (6%)
  other arithmetic  2.78 us (1%)
    all_to_all x1, waiting for transfers between devices, body(): lax.all_to_all(outgoing, 'dp', split_axis=0, concat_axis=0, tiled=True)  46.5 us
    unnamed x14, local copies, waits for them, and re-layouts  45.6 us
    all_gather x1, blocking collectives, body(): lax.all_gather(attention, 'dp', axis=0, tiled=True)  25.4 us
    psum x1, blocking collectives, body(): summed = lax.psum(partial_sums, 'tensor')  21.2 us
    dot_general x1, matrix products, body(): jnp.dot(hit_table.astype(jnp.bfloat16), arrived.reshape(holding_rows, -1)...  10.8 us
    gather x1, local copies, waits for them, and re-layouts, body(): gathered = new_pages[block_table]  9.14 us
    gather x1, local copies, waits for them, and re-layouts, body(): picked = flat_pages[move_list[0]]  7.81 us
    all_to_all x1, starting transfers between devices, body(): lax.all_to_all(slot_tags, 'dp', split_axis=0, concat_axis=0, tiled=True)  6.37 us
  transfers between devices with their start and end apart: 2, of which 1 were waited for; matrix products, arithmetic and copies ran while one was open for 17% of the time, Pallas kernels for 0%

commit v1 on v0

--- a/solution.py
+++ b/solution.py
@@ -78,11 +78,24 @@
     attention = mixed_heads.reshape(seq_here, local_heads * group_size * head_dim).astype(
         jnp.bfloat16
     )
-    partial_sums = jnp.dot(
-        lax.all_gather(attention, "dp", axis=0, tiled=True),
-        out_weight,
-        preferred_element_type=jnp.float32,
-    )
+
+    def _draw_slices(mine_x, comm_axis="dp"):
+        fresh = lax.axis_size(comm_axis)
+        step_out, val, carry_in = (fresh, lax.axis_index(comm_axis), mine_x.shape[0])
+        items = [dev_i * step_out if i == 0 else dev_i for i, dev_i in enumerate(mine_x.shape)]
+        near = lax.dynamic_update_slice_in_dim(
+            jnp.zeros(items, mine_x.dtype), mine_x, val * carry_in, axis=0
+        )
+        for ix in range(1, step_out):
+            reply = range(step_out)
+            newest = map(lambda i: (i, (i + 1) % step_out), reply)
+            mine_x = lax.ppermute(mine_x, comm_axis, list(newest))
+            near = lax.dynamic_update_slice_in_dim(
+                near, mine_x, (val - ix) % step_out * carry_in, axis=0
+            )
+        return near
+
+    partial_sums = jnp.dot(_draw_slices(attention), out_weight, preferred_element_type=jnp.float32)
     summed = lax.psum(partial_sums, "tensor")
     return (new_pages, summed.astype(jnp.bfloat16))
 

time: 196 us -> 211 us (1.077)
  waiting for transfers between devices: 46.5 us -> 82.5 us
  blocking collectives: 46.6 us -> 23.9 us
  starting transfers between devices: 11.8 us -> 14 us
    ppermute x0 -> x7, waiting for transfers between devices: none -> 36 us  [_draw_slices(): mine_x = lax.ppermute(mine_x, comm_axis, list(newest))]
    all_gather x1 -> x0, blocking collectives: 25.4 us -> none  [body(): lax.all_gather(attention, 'dp', axis=0, tiled=True)]
    psum x1, blocking collectives: 21.2 us -> 23.9 us  [body(): summed = lax.psum(partial_sums, 'tensor')]
    ppermute x0 -> x7, starting transfers between devices: none -> 2.17 us  [_draw_slices(): mine_x = lax.ppermute(mine_x, comm_axis, list(newest))]
  transfers between devices with their start and end apart: 2 -> 9, of which waited for: 1 -> 8; matrix products, arithmetic and copies ran while one was open for 17% -> 16% of each run, Pallas kernels for 0% -> 0%
where the time goes in v1:
time: 211 us
  waiting for transfers between devices  82.5 us (39%)
  local copies, waits for them, and re-layouts  67.3 us (32%)
  blocking collectives  23.9 us (11%)
  matrix products  18.6 us (9%)
  starting transfers between devices  14 us (7%)
  other arithmetic  2.78 us (1%)
    all_to_all x1, waiting for transfers between devices, body(): lax.all_to_all(outgoing, 'dp', split_axis=0, concat_axis=0, tiled=True)  46.5 us
    unnamed x14, local copies, waits for them, and re-layouts  45.6 us
    ppermute x7, waiting for transfers between devices, _draw_slices(): mine_x = lax.ppermute(mine_x, comm_axis, list(newest))  36 us
    psum x1, blocking collectives, body(): summed = lax.psum(partial_sums, 'tensor')  23.9 us
    dot_general x1, matrix products, body(): jnp.dot(hit_table.astype(jnp.bfloat16), arrived.reshape(holding_rows, -1)...  10.8 us
    gather x1, local copies, waits for them, and re-layouts, body(): gathered = new_pages[block_table]  9.14 us
    gather x1, local copies, waits for them, and re-layouts, body(): picked = flat_pages[move_list[0]]  7.81 us
    all_to_all x1, starting transfers between devices, body(): lax.all_to_all(slot_tags, 'dp', split_axis=0, concat_axis=0, tiled=True)  6.37 us
  transfers between devices with their start and end apart: 9, of which 8 were waited for; matrix products, arithmetic and copies ran while one was open for 16% of the time, Pallas kernels for 0%

profile of v1, /device:TPU:1, one launch (start us, length us, event | category | flops | bytes accessed | tf_op | source)
XLA Modules:
  0.0 210.5 jit_solution(10932892603627373487)
XLA Ops:
  0.6 0.0 copy-start
  0.6 0.7 slice_bitcast_fusion
  2.0 0.2 convert_reduce_fusion
  2.2 0.7 add_select_fusion
  2.8 0.1 select_reduce_fusion
  3.0 0.7 convert_element_type.79
  3.7 6.4 %all-to-all-start = ((bf16[8,2,1]{1,2,0:T(2,128)(2,1)}), bf16[8,2,1]{1,2,0:T(2,128)(2,1)S(1)}, u32[]{:S(2)}, u32[]{:S(2)}) async-start(bf16[8,2,1]{1,2,0:T(2,128)(2,1)} %convert_element_type.79), calls=%async_computation | async-start | bytes 8192 | tf_op jit(solution)/shard_map/all_to_all | solution.py:41
  10.0 0.7 fusion.16
  10.7 8.8 %pad.2 = bf16[72,512,128]{2,1,0:T(8,128)(2,1)} pad(bf16[70,512,128]{2,1,0:T(8,128)(2,1)} %bitcast.71, bf16[]{:T(256)} %constant.76.clone.1), padding=0_2x0_0x0_0 | pad | bytes 18612226
  19.5 13.8 %copy.21 = bf16[9,8,512,128]{3,1,2,0:T(8,128)(2,1)} copy(bf16[9,8,512,128]{3,2,1,0:T(8,128)(2,1)} %bitcast.64) | data formatting | bytes 18874368
  33.3 7.8 %gather_fusion = bf16[12,65536]{1,0:T(8,128)(2,1)S(1)} fusion(bf16[70,65536]{1,0:T(8,128)(2,1)} %bitcast.61, s32[1024]{0:T(1024)S(1)} %pad_clamp_fusion.1), kind=kCustom, calls=%fused_computation | custom fusion | bytes 3145776 | tf_op jit(solution)/shard_map/gather | solution.py:31
  41.1 0.7 fusion.4
  41.8 0.0 copy-start.1
  41.8 0.0 copy-start.2
  41.8 1.9 copy.22
  43.7 0.0 all-to-all-done
  43.7 5.4 %all-to-all-start.1 = ((bf16[16,2,2,128,128]{4,3,2,1,0:T(8,128)(2,1)}), bf16[16,2,2,128,128]{4,3,2,1,0:T(8,128)(2,1)S(1)}, u32[]{:S(2)}, u32[]{:S(2)}) async-start(bf16[16,2,2,128,128]{4,3,2,1,0:T(8,128)(2,1)} %bitcast.24), calls=%async_computation.1 | async-start | bytes 4194304 | tf_op jit(solution)/shard_map/all_to_all | solution.py:40
  49.2 0.1 reshape.158
  49.3 0.1 iota_compare_fusion
  49.4 0.1 convert_element_type.72
  49.4 0.1 fusion.12
  49.5 46.5 %all-to-all-done.1 = bf16[16,2,2,128,128]{4,3,2,1,0:T(8,128)(2,1)S(1)} async-done(((bf16[16,2,2,128,128]{4,3,2,1,0:T(8,128)(2,1)}), bf16[16,2,2,128,128]{4,3,2,1,0:T(8,128)(2,1)S(1)}, u32[]{:S(2)}, u32[]{:S(2)}) %all-to-all-start.1) | async-done | bytes 2097184 | tf_op jit(solution)/shard_map/all_to_all | solution.py:40
  96.0 10.8 %fusion.1 = bf16[70,65536]{1,0:T(8,128)(2,1)} fusion(bf16[70,65536]{1,0:T(8,128)(2,1)} %bitcast.62, pred[70]{0:T(512)(128)(4,1)S(1)} %fusion.12, bf16[2,8,512,128]{3,2,1,0:T(8,128)(2,1)S(1)} %bitcast.72, s32[16]{0:T(128)S(1)} %convert_element_type.72), kind=kOutput, calls=%fused_computation.4 | convolution fusion | flops 155976800 | bytes 20447366 | tf_op jit(solution)/shard_map/dot_general | solution.py:45
  106.8 9.9 %copy.24 = bf16[9,8,512,128]{3,2,1,0:T(8,128)(2,1)} copy(bf16[9,8,512,128]{3,1,2,0:T(8,128)(2,1)} %bitcast.63) | data formatting | bytes 18874368
  116.7 8.4 %slice.29 = bf16[70,512,128]{2,1,0:T(8,128)(2,1)} slice(bf16[72,512,128]{2,1,0:T(8,128)(2,1)} %bitcast.65), slice={[0:70], [0:512], [0:128]} | slice | bytes 18350080
  125.1 9.1 %gather_fusion.1 = bf16[64,2,2,128,128]{4,3,2,1,0:T(8,128)(2,1)} fusion(bf16[70,2,2,128,128]{4,3,2,1,0:T(8,128)(2,1)} %bitcast.66, s32[1024]{0:T(1024)S(1)} %pad_clamp_fusion), kind=kCustom, calls=%fused_computation.1 | custom fusion | bytes 16777472 | tf_op jit(solution)/shard_map/gather | solution.py:57
  134.2 3.8 %fusion.17 = (bf16[8,8,2,1,128,128]{5,4,3,2,1,0:T(8,128)(2,1)S(1)}, bf16[8,8,2,1,128,128]{5,4,3,2,1,0:T(8,128)(2,1)S(1)}) fusion(bf16[8,8,2,2,128,128]{5,4,3,2,1,0:T(8,128)(2,1)} %bitcast.68), kind=kLoop, calls=%fused_computation.49 | loop fusion | bytes 16777216 | tf_op jit(solution)/shard_map/slice | solution.py:58
  138.1 0.6 copy.19
  138.7 1.2 fusion.8
  139.8 0.3 fusion.18
  140.1 2.2 %copy.20 = bf16[8,8,2,1,128,128]{5,4,1,2,0,3:T(8,128)(2,1)} copy(bf16[8,8,2,1,128,128]{5,4,3,2,1,0:T(8,128)(2,1)S(1)} %get-tuple-element.3) | data formatting | bytes 8388608
  142.3 2.9 %fusion.9 = bf16[1,8,16,128]{3,2,1,0:T(8,128)(2,1)S(1)} fusion(bf16[8,2,1024,128]{3,2,1,0:T(8,128)(2,1)} %bitcast.69, f32[8,2,8]{2,1,0:T(2,128)S(1)} %fusion.18, f32[8,2,8,1024]{3,2,1,0:T(8,128)S(1)} %fusion.8), kind=kOutput, calls=%fused_computation.15 | convolution fusion | flops 33965184 | bytes 4751872 | tf_op jit(solution)/shard_map/skgt,sktd->skgd/dot_general | solution.py:75
  145.3 2.2 %collective-permute-start = (bf16[8,2048]{1,0:T(8,128)(2,1)S(1)}, bf16[8,2048]{1,0:T(8,128)(2,1)S(1)}, u32[]{:S(2)}, u32[]{:S(2)}) collective-permute-start(bf16[8,2048]{1,0:T(8,128)(2,1)S(1)} %bitcast.73), channel_id=1, source_target_pairs={{0,4},{4,8},{8,12},{12,16},{16,20},{20,24},{24,28},{28,0},{1,5},{5... | collective-permute-start | bytes 98312 | tf_op jit(solution)/shard_map/ppermute | solution.py:92
  147.5 3.3 %collective-permute-done = bf16[8,2048]{1,0:T(8,128)(2,1)S(1)} collective-permute-done((bf16[8,2048]{1,0:T(8,128)(2,1)S(1)}, bf16[8,2048]{1,0:T(8,128)(2,1)S(1)}, u32[]{:S(2)}, u32[]{:S(2)}) %collective-permute-start) | collective-permute-done | bytes 32800 | tf_op jit(solution)/shard_map/ppermute | solution.py:92
  150.8 0.0 collective-permute-start.1
  150.8 5.5 %collective-permute-done.1 = bf16[8,2048]{1,0:T(8,128)(2,1)S(1)} collective-permute-done((bf16[8,2048]{1,0:T(8,128)(2,1)S(1)}, bf16[8,2048]{1,0:T(8,128)(2,1)S(1)}, u32[]{:S(2)}, u32[]{:S(2)}) %collective-permute-start.1) | collective-permute-done | bytes 32800 | tf_op jit(solution)/shard_map/ppermute | solution.py:92
  156.3 0.0 collective-permute-start.2
  156.3 5.5 %collective-permute-done.2 = bf16[8,2048]{1,0:T(8,128)(2,1)S(1)} collective-permute-done((bf16[8,2048]{1,0:T(8,128)(2,1)S(1)}, bf16[8,2048]{1,0:T(8,128)(2,1)S(1)}, u32[]{:S(2)}, u32[]{:S(2)}) %collective-permute-start.2) | collective-permute-done | bytes 32800 | tf_op jit(solution)/shard_map/ppermute | solution.py:92
  161.7 0.0 collective-permute-start.3
  161.7 5.5 %collective-permute-done.3 = bf16[8,2048]{1,0:T(8,128)(2,1)S(1)} collective-permute-done((bf16[8,2048]{1,0:T(8,128)(2,1)S(1)}, bf16[8,2048]{1,0:T(8,128)(2,1)S(1)}, u32[]{:S(2)}, u32[]{:S(2)}) %collective-permute-start.3) | collective-permute-done | bytes 32800 | tf_op jit(solution)/shard_map/ppermute | solution.py:92
  167.2 0.0 collective-permute-start.4
  167.2 5.5 %collective-permute-done.4 = bf16[8,2048]{1,0:T(8,128)(2,1)S(1)} collective-permute-done((bf16[8,2048]{1,0:T(8,128)(2,1)S(1)}, bf16[8,2048]{1,0:T(8,128)(2,1)S(1)}, u32[]{:S(2)}, u32[]{:S(2)}) %collective-permute-start.4) | collective-permute-done | bytes 32800 | tf_op jit(solution)/shard_map/ppermute | solution.py:92
  172.6 0.0 collective-permute-start.5
  172.7 5.5 %collective-permute-done.5 = bf16[8,2048]{1,0:T(8,128)(2,1)S(1)} collective-permute-done((bf16[8,2048]{1,0:T(8,128)(2,1)S(1)}, bf16[8,2048]{1,0:T(8,128)(2,1)S(1)}, u32[]{:S(2)}, u32[]{:S(2)}) %collective-permute-start.5) | collective-permute-done | bytes 32800 | tf_op jit(solution)/shard_map/ppermute | solution.py:92
  178.1 0.0 collective-permute-start.6
  178.1 5.5 %collective-permute-done.6 = bf16[8,2048]{1,0:T(8,128)(2,1)S(1)} collective-permute-done((bf16[8,2048]{1,0:T(8,128)(2,1)S(1)}, bf16[8,2048]{1,0:T(8,128)(2,1)S(1)}, u32[]{:S(2)}, u32[]{:S(2)}) %collective-permute-start.6) | collective-permute-done | bytes 32800 | tf_op jit(solution)/shard_map/ppermute | solution.py:92
  183.6 3.0 %fusion.19 = f32[64,1024]{1,0:T(8,128)S(1)} fusion(bf16[64,2048]{1,0:T(8,128)(2,1)S(1)} %constant_dynamic-update-slice_fusion, bf16[2048,1024]{1,0:T(8,128)(2,1)} %param.13), kind=kOutput, calls=%fused_computation.51 | convolution fusion | flops 268435456 | bytes 4718592 | tf_op jit(solution)/shard_map/dot_general | solution.py:98
  186.6 23.9 %all-reduce.1 = bf16[64,1024]{1,0:T(8,128)(2,1)} all-reduce(f32[64,1024]{1,0:T(8,128)S(1)} %fusion.19), channel_id=1, replica_groups=mesh['dp'=8,'tensor'=4] {'tensor'}, use_global_device_ids=true, to_apply=%region_5.6 | all-reduce | flops 65536 | bytes 393216 | tf_op jit(solution)/shard_map/psum | solution.py:99
  (19 shorter events, 0.1 us)
Async XLA Ops:
  0.6 138.0 %copy-start = (bf16[8,16,128]{2,1,0:T(8,128)(2,1)S(1)}, bf16[8,16,128]{2,1,0:T(8,128)(2,1)}, u32[]{:S(2)}) copy-start(bf16[8,16,128]{2,1,0:T(8,128)(2,1)} %param.7) | copy-start | bytes 98308
  3.7 40.1 %all-to-all-start = ((bf16[8,2,1]{1,2,0:T(2,128)(2,1)}), bf16[8,2,1]{1,2,0:T(2,128)(2,1)S(1)}, u32[]{:S(2)}, u32[]{:S(2)}) async-start(bf16[8,2,1]{1,2,0:T(2,128)(2,1)} %convert_element_type.79), calls=%async_computation | async-start | bytes 8192 | tf_op jit(solution)/shard_map/all_to_all | solution.py:41
  41.8 7.3 %copy-start.1 = (s32[8,8]{1,0:T(8,128)S(1)}, s32[8,8]{1,0:T(8,128)}, u32[]{:S(2)}) copy-start(s32[8,8]{1,0:T(8,128)} %param.11) | copy-start | bytes 772
  41.8 7.4 %copy-start.2 = (s32[8]{0:T(128)S(1)}, s32[8]{0:T(128)}, u32[]{:S(2)}) copy-start(s32[8]{0:T(128)} %param.12) | copy-start | bytes 100
  43.7 52.3 %all-to-all-start.1 = ((bf16[16,2,2,128,128]{4,3,2,1,0:T(8,128)(2,1)}), bf16[16,2,2,128,128]{4,3,2,1,0:T(8,128)(2,1)S(1)}, u32[]{:S(2)}, u32[]{:S(2)}) async-start(bf16[16,2,2,128,128]{4,3,2,1,0:T(8,128)(2,1)} %bitcast.24), calls=%async_computation.1 | async-start | bytes 4194304 | tf_op jit(solution)/shard_map/all_to_all | solution.py:40
  145.3 5.5 %collective-permute-start = (bf16[8,2048]{1,0:T(8,128)(2,1)S(1)}, bf16[8,2048]{1,0:T(8,128)(2,1)S(1)}, u32[]{:S(2)}, u32[]{:S(2)}) collective-permute-start(bf16[8,2048]{1,0:T(8,128)(2,1)S(1)} %bitcast.73), channel_id=1, source_target_pairs={{0,4},{4,8},{8,12},{12,16},{16,20},{20,24},{24,28},{28,0},{1,5},{5... | collective-permute-start | bytes 98312 | tf_op jit(solution)/shard_map/ppermute | solution.py:92
  150.8 5.5 %collective-permute-start.1 = (bf16[8,2048]{1,0:T(8,128)(2,1)S(1)}, bf16[8,2048]{1,0:T(8,128)(2,1)S(1)}, u32[]{:S(2)}, u32[]{:S(2)}) collective-permute-start(bf16[8,2048]{1,0:T(8,128)(2,1)S(1)} %collective-permute-done), channel_id=1, source_target_pairs={{0,4},{4,8},{8,12},{12,16},{16,20},{20,24},{24,28},{28,0},{1,5},{5... | collective-permute-start | bytes 98312 | tf_op jit(solution)/shard_map/ppermute | solution.py:92
  156.3 5.5 %collective-permute-start.2 = (bf16[8,2048]{1,0:T(8,128)(2,1)S(1)}, bf16[8,2048]{1,0:T(8,128)(2,1)S(1)}, u32[]{:S(2)}, u32[]{:S(2)}) collective-permute-start(bf16[8,2048]{1,0:T(8,128)(2,1)S(1)} %collective-permute-done.1), channel_id=1, source_target_pairs={{0,4},{4,8},{8,12},{12,16},{16,20},{20,24},{24,28},{28,0},{1,5},{5... | collective-permute-start | bytes 98312 | tf_op jit(solution)/shard_map/ppermute | solution.py:92
  161.7 5.5 %collective-permute-start.3 = (bf16[8,2048]{1,0:T(8,128)(2,1)S(1)}, bf16[8,2048]{1,0:T(8,128)(2,1)S(1)}, u32[]{:S(2)}, u32[]{:S(2)}) collective-permute-start(bf16[8,2048]{1,0:T(8,128)(2,1)S(1)} %collective-permute-done.2), channel_id=1, source_target_pairs={{0,4},{4,8},{8,12},{12,16},{16,20},{20,24},{24,28},{28,0},{1,5},{5... | collective-permute-start | bytes 98312 | tf_op jit(solution)/shard_map/ppermute | solution.py:92
  167.2 5.5 %collective-permute-start.4 = (bf16[8,2048]{1,0:T(8,128)(2,1)S(1)}, bf16[8,2048]{1,0:T(8,128)(2,1)S(1)}, u32[]{:S(2)}, u32[]{:S(2)}) collective-permute-start(bf16[8,2048]{1,0:T(8,128)(2,1)S(1)} %collective-permute-done.3), channel_id=1, source_target_pairs={{0,4},{4,8},{8,12},{12,16},{16,20},{20,24},{24,28},{28,0},{1,5},{5... | collective-permute-start | bytes 98312 | tf_op jit(solution)/shard_map/ppermute | solution.py:92
  172.6 5.5 %collective-permute-start.5 = (bf16[8,2048]{1,0:T(8,128)(2,1)S(1)}, bf16[8,2048]{1,0:T(8,128)(2,1)S(1)}, u32[]{:S(2)}, u32[]{:S(2)}) collective-permute-start(bf16[8,2048]{1,0:T(8,128)(2,1)S(1)} %collective-permute-done.4), channel_id=1, source_target_pairs={{0,4},{4,8},{8,12},{12,16},{16,20},{20,24},{24,28},{28,0},{1,5},{5... | collective-permute-start | bytes 98312 | tf_op jit(solution)/shard_map/ppermute | solution.py:92
  178.1 5.5 %collective-permute-start.6 = (bf16[8,2048]{1,0:T(8,128)(2,1)S(1)}, bf16[8,2048]{1,0:T(8,128)(2,1)S(1)}, u32[]{:S(2)}, u32[]{:S(2)}) collective-permute-start(bf16[8,2048]{1,0:T(8,128)(2,1)S(1)} %collective-permute-done.5), channel_id=1, source_target_pairs={{0,4},{4,8},{8,12},{12,16},{16,20},{20,24},{24,28},{28,0},{1,5},{5... | collective-permute-start | bytes 98312 | tf_op jit(solution)/shard_map/ppermute | solution.py:92
